TPU v7x, 512 devices: a whole 4x4x16 slice. The times are simulated.
512 devices in a mesh: gx: 16 (over z), gy: 32 (over x, y, core).
Axes of the slice: x: 4, y: 4, z: 16, core: 2. Of those that a mesh axis runs over, the one named last changes fastest.
Arguments:
- labels: int32 [64, 256, 128], P('gx', 'gy'), may hold values from 0 to 16, as said below
- layer_index: int32 [128], replicated, may hold values from 0 to 7
- layer_eps: float32 [8], replicated, may hold values from 1 to 12
Outputs:
- solution_block: float32 [16, 64, 256, 128], P(None, 'gx', 'gy')
- residual_block: float32 [16, 64, 256, 128], P(None, 'gx', 'gy')
Inputs may be any that keep to these rules, and one draw needn't show every extreme that they name: `labels`: 0 marks a dielectric cell; k marks a cell of conductor k.
All inputs are finite; a program needn't handle non-finite values.
Results may differ from a plain program's by a relative error of at most 0.0003.
Values sent between devices are 32-bit elements; how exact they have to be, the bound alone decides.
No kernel may reach another device: no remote copies, remote signals or barrier semaphores. Data moves between devices by JAX's collectives and lax.ppermute only.
A program may use at most 64 MiB of HBM per device.

v0:
```python
import jax
import jax.numpy as jnp
from jax import lax
from jax.sharding import PartitionSpec as P

K = 16
ITERS = 3


def extended(block, sides, width):
    for axis, dim in sides:
        count = lax.axis_size(axis)
        forward = [(i, i + 1) for i in range(count - 1)]
        backward = [(target, source) for source, target in forward]
        low = lax.ppermute(
            lax.slice_in_dim(block, block.shape[dim] - width, None, axis=dim), axis, forward
        )
        high = lax.ppermute(lax.slice_in_dim(block, 0, width, axis=dim), axis, backward)
        block = jnp.concatenate([low, block, high], axis=dim)
    return block


def coefficients(layer_index, layer_eps):
    table = (
        layer_index[:, None] == jnp.arange(layer_eps.shape[0], dtype=jnp.int32)[None, :]
    ).astype(jnp.float32)
    eps_plane = jnp.dot(
        table, layer_eps, precision=lax.Precision.HIGHEST, preferred_element_type=jnp.float32
    )
    middle = 0.5 * (eps_plane[1:] + eps_plane[:-1])
    c_down = jnp.concatenate([eps_plane[:1], middle])
    c_up = jnp.concatenate([middle, eps_plane[-1:]])
    diagonal = 4.0 * eps_plane + c_down + c_up
    return (eps_plane, c_down, c_up, diagonal)


def laplace(padded, coeffs):
    eps_plane, c_down, c_up, diagonal = coeffs
    field = padded[:, 1:-1, 1:-1]
    lateral = (
        padded[:, 2:, 1:-1] + padded[:, :-2, 1:-1] + padded[:, 1:-1, 2:] + padded[:, 1:-1, :-2]
    )
    below = jnp.pad(field[..., :-1], ((0, 0), (0, 0), (0, 0), (1, 0)))
    above = jnp.pad(field[..., 1:], ((0, 0), (0, 0), (0, 0), (0, 1)))
    return diagonal * field - eps_plane * lateral - c_down * below - c_up * above


def local_gram(left, right):
    count = left.shape[0]
    return jnp.dot(
        left.reshape(count, -1),
        right.reshape(count, -1).T,
        precision=lax.Precision.HIGHEST,
        preferred_element_type=jnp.float32,
    )


def combine_rows(coef, field):
    count = field.shape[0]
    return jnp.dot(
        coef,
        field.reshape(count, -1),
        precision=lax.Precision.HIGHEST,
        preferred_element_type=jnp.float32,
    ).reshape(field.shape)


def lower_inverse(factor):
    count = factor.shape[0]
    inverse = jnp.zeros((count, count), jnp.float32)
    unit = jnp.eye(count, dtype=jnp.float32)
    for row in range(count):
        partial_row = unit[row] - jnp.dot(factor[row], inverse, precision=lax.Precision.HIGHEST)
        inverse = inverse.at[row].set(partial_row / factor[row, row])
    return inverse


def apply_operator(search, free, coeffs):
    padded = extended(search, (("gx", 1), ("gy", 2)), 1)
    return free * laplace(padded, coeffs)


def on_device(labels, layer_index, layer_eps):
    coeffs = coefficients(layer_index, layer_eps)
    free = (labels == 0).astype(jnp.float32)
    conductor_ids = jnp.arange(1, K + 1, dtype=jnp.int32)
    excitation = (labels[None] == conductor_ids[:, None, None, None]).astype(jnp.float32)
    padded_exc = extended(excitation, (("gx", 1), ("gy", 2)), 1)
    right_side = -free * laplace(padded_exc, coeffs)
    inverse_diag = free / coeffs[3]
    solution = jnp.zeros_like(right_side)
    residual = right_side
    prev_search = None
    prev_image = None
    for step in range(ITERS):
        precond = inverse_diag * residual
        if step == 0:
            search = precond
        else:
            beta = lax.psum(local_gram(prev_image, precond), ("gx", "gy"))
            search = precond - combine_rows(beta.T, prev_search)
        image = apply_operator(search, free, coeffs)
        curvature = lax.psum(local_gram(search, image), ("gx", "gy"))
        inverse = lower_inverse(jnp.linalg.cholesky(curvature))
        prev_search = combine_rows(inverse, search)
        prev_image = combine_rows(inverse, image)
        alpha = lax.psum(local_gram(prev_search, residual), ("gx", "gy"))
        solution = solution + combine_rows(alpha.T, prev_search)
        residual = residual - combine_rows(alpha.T, prev_image)
    return (solution, residual)


def solution(mesh):
    placed = (P("gx", "gy", None), P(), P())
    return jax.shard_map(
        on_device,
        mesh=mesh,
        in_specs=placed,
        out_specs=(P(None, "gx", "gy", None), P(None, "gx", "gy", None)),
        check_vma=False,
    )
```

profile of v0, /device:TPU:1, one launch (start us, length us, event | category | flops | bytes accessed | tf_op | source)
XLA Modules:
  0.0 967.6 jit_solution(16897844907388868109)
XLA Ops:
  1.5 4.4 collective-permute-start.1
  5.9 1.3 collective-permute-start
  8.3 1.4 add_add_fusion
  9.7 1.4 collective-permute-done
  11.1 6.7 collective-permute-start.2
  17.8 1.9 collective-permute-start.3
  19.8 1.2 collective-permute-done.3
  21.2 1.9 collective-permute-start.5
  23.1 1.3 collective-permute-start.4
  24.5 5.3 collective-permute-done.4
  29.8 2.3 collective-permute-start.6
  32.1 4.7 collective-permute-start.7
  36.9 1.0 collective-permute-done.7
  38.8 113.6 %psum.56 = f32[16,16]{0,1:T(8,128)S(1)} all-reduce(f32[16,16]{0,1:T(8,128)S(1)} %convolution_bitcast_fusion.7), channel_id=1, replica_groups=mesh['gx'=16,'gy'=32] {'gx','gy'}, use_global_device_ids=true, to_apply=%region_0.1 | all-reduce | flops 256 | bytes 2048 | tf_op jit(solution)/shard_map/psum | solution.py:103
  152.5 1.5 cholesky.59
  157.5 1.4 fusion.54
  159.0 1.5 fusion.56
  160.5 1.4 fusion.58
  161.9 1.5 fusion.60
  163.4 1.5 fusion.62
  164.9 1.5 fusion.64
  166.4 1.5 fusion.66
  167.9 1.5 fusion.68
  169.5 1.4 fusion.70
  170.9 1.5 fusion.72
  172.4 1.4 fusion.74
  173.9 1.5 fusion.76
  175.3 1.4 fusion.78
  176.8 1.5 fusion.80
  179.8 98.8 %psum.57 = f32[16,16]{1,0:T(8,128)S(1)} all-reduce(f32[16,16]{1,0:T(8,128)S(1)} %fusion.176), channel_id=1, replica_groups=mesh['gx'=16,'gy'=32] {'gx','gy'}, use_global_device_ids=true, to_apply=%region_3.5 | all-reduce | flops 256 | bytes 2048 | tf_op jit(solution)/shard_map/psum | solution.py:107
  279.7 99.6 %psum.58 = f32[16,16]{1,0:T(8,128)S(1)} all-reduce(f32[16,16]{1,0:T(8,128)S(1)} %fusion.170), channel_id=1, replica_groups=mesh['gx'=16,'gy'=32] {'gx','gy'}, use_global_device_ids=true, to_apply=%region_4.6 | all-reduce | flops 256 | bytes 2048 | tf_op jit(solution)/shard_map/psum | solution.py:100
  379.8 2.8 collective-permute-start.9
  382.6 1.3 collective-permute-start.8
  384.1 3.6 collective-permute-done.8
  387.7 4.0 collective-permute-start.10
  391.7 2.5 collective-permute-start.11
  396.2 104.3 %psum.59 = f32[16,16]{0,1:T(8,128)S(1)} all-reduce(f32[16,16]{0,1:T(8,128)S(1)} %convolution_bitcast_fusion.6), channel_id=1, replica_groups=mesh['gx'=16,'gy'=32] {'gx','gy'}, use_global_device_ids=true, to_apply=%region_5.7 | all-reduce | flops 256 | bytes 2048 | tf_op jit(solution)/shard_map/psum | solution.py:103
  500.6 1.5 cholesky.70
  505.7 1.5 fusion.86
  507.2 1.5 fusion.88
  508.6 1.4 fusion.90
  510.1 1.5 fusion.92
  511.6 1.5 fusion.94
  513.1 1.5 fusion.96
  514.6 1.5 fusion.98
  516.1 1.5 fusion.100
  517.6 1.4 fusion.102
  519.0 1.5 fusion.104
  520.6 1.4 fusion.106
  522.0 1.5 fusion.108
  523.5 1.4 fusion.110
  525.0 1.5 fusion.112
  528.1 98.5 %psum.60 = f32[16,16]{1,0:T(8,128)S(1)} all-reduce(f32[16,16]{1,0:T(8,128)S(1)} %fusion.164), channel_id=1, replica_groups=mesh['gx'=16,'gy'=32] {'gx','gy'}, use_global_device_ids=true, to_apply=%region_6.8 | all-reduce | flops 256 | bytes 2048 | tf_op jit(solution)/shard_map/psum | solution.py:107
  627.7 100.0 %psum.61 = f32[16,16]{1,0:T(8,128)S(1)} all-reduce(f32[16,16]{1,0:T(8,128)S(1)} %fusion.158), channel_id=1, replica_groups=mesh['gx'=16,'gy'=32] {'gx','gy'}, use_global_device_ids=true, to_apply=%region_7.9 | all-reduce | flops 256 | bytes 2048 | tf_op jit(solution)/shard_map/psum | solution.py:100
  728.2 2.6 collective-permute-start.13
  730.8 1.3 collective-permute-start.12
  732.6 3.3 collective-permute-done.12
  735.9 4.0 collective-permute-start.14
  739.9 2.6 collective-permute-start.15
  742.7 1.0 collective-permute-done.15
  744.6 104.5 %psum.62 = f32[16,16]{0,1:T(8,128)S(1)} all-reduce(f32[16,16]{0,1:T(8,128)S(1)} %convolution_bitcast_fusion.5), channel_id=1, replica_groups=mesh['gx'=16,'gy'=32] {'gx','gy'}, use_global_device_ids=true, to_apply=%region_8.10 | all-reduce | flops 256 | bytes 2048 | tf_op jit(solution)/shard_map/psum | solution.py:103
  849.1 1.5 cholesky.81
  859.7 0.8 fusion.132
  866.7 98.5 %psum.63 = f32[16,16]{1,0:T(8,128)S(1)} all-reduce(f32[16,16]{1,0:T(8,128)S(1)} %fusion.152), channel_id=1, replica_groups=mesh['gx'=16,'gy'=32] {'gx','gy'}, use_global_device_ids=true, to_apply=%region_9.11 | all-reduce | flops 256 | bytes 2048 | tf_op jit(solution)/shard_map/psum | solution.py:107
  (165 shorter events, 38.8 us)
Async XLA Ops:
  0.6 6.6 copy-start
  1.5 5.7 copy-start.6
  1.5 8.2 collective-permute-start.1
  5.9 5.2 collective-permute-start
  8.1 1.5 copy-start.1
  11.1 8.6 collective-permute-start.2
  17.8 3.1 collective-permute-start.3
  21.2 3.2 collective-permute-start.5
  23.1 6.6 collective-permute-start.4
  24.4 132.3 %copy-start.2 = (f32[16,16]{1,0:T(8,128)}, f32[16,16]{1,0:T(8,128)S(1)}, u32[]{:S(2)}) copy-start(f32[16,16]{1,0:T(8,128)S(1)} %fusion.220) | copy-start | bytes 3076
  29.8 7.1 collective-permute-start.6
  32.1 5.9 collective-permute-start.7
  155.3 1.4 copy-start.4
  379.8 4.3 collective-permute-start.9
  382.6 5.0 collective-permute-start.8
  387.7 6.9 collective-permute-start.10
  391.7 3.6 collective-permute-start.11
  503.4 1.4 copy-start.5
  503.4 0.7 copy-start.3
  728.2 4.3 collective-permute-start.13
  730.8 5.0 collective-permute-start.12
  735.9 6.8 collective-permute-start.14
  739.9 3.8 collective-permute-start.15
where the time goes:
time: 971 us; the launch traced here: 968 us
  blocking collectives  818 us (84%)
  matrix products  66.8 us (7%)
  starting transfers between devices  45.5 us (5%)
  waiting for transfers between devices  17.5 us (2%)
  other arithmetic  12.7 us (1%)
    psum x3, blocking collectives, on_device(): curvature = lax.psum(local_gram(search, image), ('gx', 'gy'))  322 us
    psum x3, blocking collectives, on_device(): alpha = lax.psum(local_gram(prev_search, residual), ('gx', 'gy'))  296 us
    psum x2, blocking collectives, on_device(): beta = lax.psum(local_gram(prev_image, precond), ('gx', 'gy'))  200 us
    dot_general x48, matrix products, lower_inverse(): jnp.dot(factor[row], inverse, precision=lax.Precision.HIGHEST)  55.8 us
    ppermute x8, starting transfers between devices, extended(): lax.ppermute(lax.slice_in_dim(block, block.shape[dim] - width, None, axis...  23.4 us
    ppermute x8, starting transfers between devices, extended(): lax.ppermute(lax.slice_in_dim(block, 0, width, axis=dim), axis, backward)  22.1 us
  transfers between devices with their start and end apart: 16, of which 8 were waited for; matrix products, arithmetic and copies ran while one was open for 0% of the time, Pallas kernels for 0%

commit v1 on v0

--- a/solution.py
+++ b/solution.py
@@ -5,6 +5,12 @@
 
 K = 16
 ITERS = 3
+
+
+def mix_indices(message):
+    for ix in ("gy", "gx"):
+        message = jax.lax.psum(message, ix)
+    return message
 
 
 def extended(block, sides, width):
@@ -100,7 +106,7 @@
             beta = lax.psum(local_gram(prev_image, precond), ("gx", "gy"))
             search = precond - combine_rows(beta.T, prev_search)
         image = apply_operator(search, free, coeffs)
-        curvature = lax.psum(local_gram(search, image), ("gx", "gy"))
+        curvature = mix_indices(local_gram(search, image))
         inverse = lower_inverse(jnp.linalg.cholesky(curvature))
         prev_search = combine_rows(inverse, search)
         prev_image = combine_rows(inverse, image)

time: 971 us -> 938 us (0.966)
  blocking collectives: 818 us -> 786 us
    psum x3 -> x6, blocking collectives: 322 us -> 264 us  [mix_indices(): message = jax.lax.psum(message, ix)]
    psum x3, blocking collectives: 296 us -> 318 us  [on_device(): alpha = lax.psum(local_gram(prev_search, residual), ('gx', 'gy'))]
where the time goes in v1:
time: 938 us; the launch traced here: 934 us
  blocking collectives  786 us (84%)
  matrix products  67 us (7%)
  starting transfers between devices  44.1 us (5%)
  waiting for transfers between devices  17.5 us (2%)
  other arithmetic  12.7 us (1%)
    psum x3, blocking collectives, on_device(): alpha = lax.psum(local_gram(prev_search, residual), ('gx', 'gy'))  318 us
    psum x6, blocking collectives, mix_indices(): message = jax.lax.psum(message, ix)  264 us
    psum x2, blocking collectives, on_device(): beta = lax.psum(local_gram(prev_image, precond), ('gx', 'gy'))  203 us
    dot_general x48, matrix products, lower_inverse(): jnp.dot(factor[row], inverse, precision=lax.Precision.HIGHEST)  56 us
    ppermute x8, starting transfers between devices, extended(): lax.ppermute(lax.slice_in_dim(block, 0, width, axis=dim), axis, backward)  22.1 us
    ppermute x8, starting transfers between devices, extended(): lax.ppermute(lax.slice_in_dim(block, block.shape[dim] - width, None, axis...  22 us
  transfers between devices with their start and end apart: 16, of which 8 were waited for; matrix products, arithmetic and copies ran while one was open for 0% of the time, Pallas kernels for 0%

profile of v1, /device:TPU:1, one launch (start us, length us, event | category | flops | bytes accessed | tf_op | source)
XLA Modules:
  0.0 934.3 jit_solution(5239269594201794985)
XLA Ops:
  1.5 4.4 collective-permute-start.1
  5.9 1.3 collective-permute-start
  8.3 1.4 add_add_fusion
  9.7 1.4 collective-permute-done
  11.1 6.7 collective-permute-start.2
  17.8 1.9 collective-permute-start.3
  19.8 1.2 collective-permute-done.3
  21.2 1.9 collective-permute-start.5
  23.1 1.3 collective-permute-start.4
  24.5 5.3 collective-permute-done.4
  29.8 2.3 collective-permute-start.6
  32.1 4.7 collective-permute-start.7
  38.8 64.4 %psum.77 = f32[16,16]{0,1:T(8,128)S(1)} all-reduce(f32[16,16]{0,1:T(8,128)S(1)} %convolution_bitcast_fusion.7), channel_id=1, replica_groups=mesh['gx'=16,'gy'=32] {'gy'}, use_global_device_ids=true, to_apply=%region_0.1 | all-reduce | flops 256 | bytes 2048 | tf_op jit(solution)/shard_map/psum | solution.py:12
  103.3 27.8 %psum.78 = f32[16,16]{0,1:T(8,128)S(1)} all-reduce(f32[16,16]{0,1:T(8,128)S(1)} %psum.77), channel_id=1, replica_groups=mesh['gx'=16,'gy'=32] {'gx'}, use_global_device_ids=true, to_apply=%region_1.2 | all-reduce | flops 256 | bytes 2048 | tf_op jit(solution)/shard_map/psum | solution.py:12
  131.1 1.5 cholesky.59
  136.1 1.5 fusion.54
  137.6 1.5 fusion.56
  139.1 1.5 fusion.58
  140.6 1.5 fusion.60
  142.1 1.5 fusion.62
  143.7 1.4 fusion.64
  145.1 1.5 fusion.66
  146.6 1.4 fusion.68
  148.1 1.5 fusion.70
  149.5 1.4 fusion.72
  151.0 1.5 fusion.74
  152.5 1.5 fusion.76
  154.0 1.4 fusion.78
  155.4 1.5 fusion.80
  158.5 106.9 %psum.79 = f32[16,16]{1,0:T(8,128)S(1)} all-reduce(f32[16,16]{1,0:T(8,128)S(1)} %fusion.176), channel_id=1, replica_groups=mesh['gx'=16,'gy'=32] {'gx','gy'}, use_global_device_ids=true, to_apply=%region_4.6 | all-reduce | flops 256 | bytes 2048 | tf_op jit(solution)/shard_map/psum | solution.py:113
  266.5 101.6 %psum.80 = f32[16,16]{1,0:T(8,128)S(1)} all-reduce(f32[16,16]{1,0:T(8,128)S(1)} %fusion.170), channel_id=1, replica_groups=mesh['gx'=16,'gy'=32] {'gx','gy'}, use_global_device_ids=true, to_apply=%region_5.7 | all-reduce | flops 256 | bytes 2048 | tf_op jit(solution)/shard_map/psum | solution.py:106
  368.7 1.7 collective-permute-start.9
  370.4 1.3 collective-permute-start.8
  371.9 3.6 collective-permute-done.8
  375.5 4.0 collective-permute-start.10
  379.5 2.8 collective-permute-start.11
  384.4 62.3 %psum.81 = f32[16,16]{0,1:T(8,128)S(1)} all-reduce(f32[16,16]{0,1:T(8,128)S(1)} %convolution_bitcast_fusion.6), channel_id=1, replica_groups=mesh['gx'=16,'gy'=32] {'gy'}, use_global_device_ids=true, to_apply=%region_6.8 | all-reduce | flops 256 | bytes 2048 | tf_op jit(solution)/shard_map/psum | solution.py:12
  446.7 23.7 %psum.82 = f32[16,16]{0,1:T(8,128)S(1)} all-reduce(f32[16,16]{0,1:T(8,128)S(1)} %psum.81), channel_id=1, replica_groups=mesh['gx'=16,'gy'=32] {'gx'}, use_global_device_ids=true, to_apply=%region_7.9 | all-reduce | flops 256 | bytes 2048 | tf_op jit(solution)/shard_map/psum | solution.py:12
  470.5 1.5 cholesky.70
  475.5 1.5 fusion.86
  477.0 1.5 fusion.88
  478.5 1.5 fusion.90
  480.0 1.5 fusion.92
  481.5 1.5 fusion.94
  483.0 1.4 fusion.96
  484.4 1.5 fusion.98
  486.0 1.4 fusion.100
  487.4 1.5 fusion.102
  488.9 1.4 fusion.104
  490.4 1.5 fusion.106
  491.9 1.5 fusion.108
  493.4 1.4 fusion.110
  494.8 1.5 fusion.112
  498.0 105.6 %psum.83 = f32[16,16]{1,0:T(8,128)S(1)} all-reduce(f32[16,16]{1,0:T(8,128)S(1)} %fusion.164), channel_id=1, replica_groups=mesh['gx'=16,'gy'=32] {'gx','gy'}, use_global_device_ids=true, to_apply=%region_8.10 | all-reduce | flops 256 | bytes 2048 | tf_op jit(solution)/shard_map/psum | solution.py:113
  604.7 101.6 %psum.84 = f32[16,16]{1,0:T(8,128)S(1)} all-reduce(f32[16,16]{1,0:T(8,128)S(1)} %fusion.158), channel_id=1, replica_groups=mesh['gx'=16,'gy'=32] {'gx','gy'}, use_global_device_ids=true, to_apply=%region_9.11 | all-reduce | flops 256 | bytes 2048 | tf_op jit(solution)/shard_map/psum | solution.py:106
  706.9 1.7 collective-permute-start.13
  708.6 1.3 collective-permute-start.12
  710.4 3.3 collective-permute-done.12
  713.7 4.0 collective-permute-start.14
  717.7 2.8 collective-permute-start.15
  722.6 62.3 %psum.85 = f32[16,16]{0,1:T(8,128)S(1)} all-reduce(f32[16,16]{0,1:T(8,128)S(1)} %convolution_bitcast_fusion.5), channel_id=1, replica_groups=mesh['gx'=16,'gy'=32] {'gy'}, use_global_device_ids=true, to_apply=%region_10.12 | all-reduce | flops 256 | bytes 2048 | tf_op jit(solution)/shard_map/psum | solution.py:12
  784.9 23.7 %psum.86 = f32[16,16]{0,1:T(8,128)S(1)} all-reduce(f32[16,16]{0,1:T(8,128)S(1)} %psum.85), channel_id=1, replica_groups=mesh['gx'=16,'gy'=32] {'gx'}, use_global_device_ids=true, to_apply=%region_11.13 | all-reduce | flops 256 | bytes 2048 | tf_op jit(solution)/shard_map/psum | solution.py:12
  808.7 1.5 cholesky.81
  826.3 105.6 %psum.87 = f32[16,16]{1,0:T(8,128)S(1)} all-reduce(f32[16,16]{1,0:T(8,128)S(1)} %fusion.152), channel_id=1, replica_groups=mesh['gx'=16,'gy'=32] {'gx','gy'}, use_global_device_ids=true, to_apply=%region_12.14 | all-reduce | flops 256 | bytes 2048 | tf_op jit(solution)/shard_map/psum | solution.py:113
  (168 shorter events, 41.8 us)
Async XLA Ops:
  0.6 6.6 copy-start
  1.5 5.7 copy-start.6
  1.5 8.2 collective-permute-start.1
  5.9 5.2 collective-permute-start
  8.1 1.5 copy-start.1
  11.1 8.6 collective-permute-start.2
  17.8 3.1 collective-permute-start.3
  21.2 3.2 collective-permute-start.5
  23.1 6.6 collective-permute-start.4
  24.4 110.9 %copy-start.2 = (f32[16,16]{1,0:T(8,128)}, f32[16,16]{1,0:T(8,128)S(1)}, u32[]{:S(2)}) copy-start(f32[16,16]{1,0:T(8,128)S(1)} %fusion.220) | copy-start | bytes 3076
  29.8 7.1 collective-permute-start.6
  32.1 5.9 collective-permute-start.7
  133.9 1.5 copy-start.4
  368.7 3.2 collective-permute-start.9
  370.4 5.0 collective-permute-start.8
  375.5 7.3 collective-permute-start.10
  379.5 4.0 collective-permute-start.11
  473.2 1.5 copy-start.5
  473.3 0.7 copy-start.3
  706.9 3.5 collective-permute-start.13
  708.6 5.0 collective-permute-start.12
  713.7 7.0 collective-permute-start.14
  717.7 4.0 collective-permute-start.15
